TPU v7x, 128 devices: a whole 4x4x4 slice. The times are simulated.
128 devices in a mesh: fsdp: 16 (over x_lo, y, core), tp: 8 (over x_hi, z).
Axes of the slice: x: 4 (x_hi: 2, x_lo: 2; x = x_hi * 2 + x_lo), y: 4, z: 4, core: 2. Of those that a mesh axis runs over, the one named last changes fastest.
Arguments:
- tokens: bfloat16 [16384, 2048], P(('fsdp', 'tp')), may hold values from -6 to 6
- grad_out: bfloat16 [16384, 2048], P(('fsdp', 'tp')), may hold values from -6 to 6
- adapter_ids: int32 [16], P('fsdp'), may hold values from 0 to 7
- first_gain: float32 [2048], replicated, may hold values from 0.1 to 1.9
- first_shift: float32 [2048], replicated, may hold values from -4 to 4
- joined_weight: bfloat16 [2048, 6144], P('fsdp', 'tp'), may hold values from -0.125 to 0.125
- joined_bias: float32 [6144], P('tp'), may hold values from -4 to 4
- dense_weight: bfloat16 [2048, 2048], P('tp', 'fsdp'), may hold values from -0.5 to 0.5
- dense_bias: float32 [2048], replicated, may hold values from -4 to 4
- second_gain: float32 [2048], replicated, may hold values from 0.1 to 1.9
- second_shift: float32 [2048], replicated, may hold values from -4 to 4
- up_weight: bfloat16 [2048, 8192], P('fsdp', 'tp'), may hold values from -0.125 to 0.125
- up_bias: float32 [8192], P('tp'), may hold values from -6 to 6
- down_weight: bfloat16 [8192, 2048], P('tp', 'fsdp'), may hold values from -0.125 to 0.125
- down_bias: float32 [2048], replicated, may hold values from -4 to 4
- joined_adapt_in: bfloat16 [8, 2048, 16], replicated, may hold values from -0.125 to 0.125
- joined_adapt_out: bfloat16 [8, 16, 6144], P(None, None, 'tp'), may hold values from -2 to 2
- dense_adapt_in: bfloat16 [8, 2048, 16], P(None, 'tp'), may hold values from -0.5 to 0.5
- dense_adapt_out: bfloat16 [8, 16, 2048], replicated, may hold values from -2 to 2
- up_adapt_in: bfloat16 [8, 2048, 16], replicated, may hold values from -0.125 to 0.125
- up_adapt_out: bfloat16 [8, 16, 8192], P(None, None, 'tp'), may hold values from -2 to 2
- down_adapt_in: bfloat16 [8, 8192, 16], P(None, 'tp'), may hold values from -0.125 to 0.125
- down_adapt_out: bfloat16 [8, 16, 2048], replicated, may hold values from -2 to 2
Outputs:
- layer_out: bfloat16 [16384, 2048], P(('fsdp', 'tp'))
- grad_tokens: float32 [16384, 2048], P(('fsdp', 'tp'))
- grad_joined_in: float32 [8, 2048, 16], replicated
- grad_joined_out: float32 [8, 16, 6144], P(None, None, 'tp')
- grad_dense_in: float32 [8, 2048, 16], P(None, 'tp')
- grad_dense_out: float32 [8, 16, 2048], replicated
- grad_up_in: float32 [8, 2048, 16], replicated
- grad_up_out: float32 [8, 16, 8192], P(None, None, 'tp')
- grad_down_in: float32 [8, 8192, 16], P(None, 'tp')
- grad_down_out: float32 [8, 16, 2048], replicated
All inputs are finite; a program needn't handle non-finite values.
Results may differ from a plain program's by a relative error of at most 0.02.
Values may be sent and summed in bfloat16 or wider, within the bound.
A program may use at most 128 MiB of HBM per device.

v0:
```python
import jax
import jax.numpy as jnp
from jax import lax
from jax.sharding import PartitionSpec as P

HEADS = 32
HEAD_DIM = 64
EPSILON = 1e-05
MASKED = -1e30
HIGHEST = lax.Precision.HIGHEST


def split_up(value, dim, size):
    before, after = (value.shape[:dim], value.shape[dim + 1 :])
    return jnp.moveaxis(value.reshape(*before, size, -1, *after), dim, 0)


def sum_at_owner(value, axis, dim):
    blocks = split_up(value, dim, lax.axis_size(axis))
    arrived = lax.all_to_all(blocks, axis, split_axis=0, concat_axis=0, tiled=True)
    return arrived.astype(jnp.float32).sum(axis=0)


def together(arrays, axis):
    ends = [0]
    for a in arrays:
        ends.append(ends[-1] + a.size)
    so_far = lax.psum(jnp.concatenate([a.ravel() for a in arrays]), axis)
    return tuple((so_far[b:e].reshape(a.shape) for a, b, e in zip(arrays, ends, ends[1:])))


def layer_norm(rows_in, gain, shift):
    row_mean = jnp.mean(rows_in, axis=-1, keepdims=True)
    centered = rows_in - row_mean
    variance = jnp.mean(centered * centered, axis=-1, keepdims=True)
    return centered * lax.rsqrt(variance + EPSILON) * gain + shift


def exact_gelu(values_in):
    return jax.nn.gelu(values_in, approximate=False)


def choose(onehot, tensor_in):
    return jnp.einsum(
        "sa,a...->s...", onehot, tensor_in, preferred_element_type=jnp.float32
    ).astype(jnp.bfloat16)


def spread(onehot, grads_in):
    return jnp.einsum("sa,s...->a...", onehot, grads_in, precision=HIGHEST)


def seq_dot(left_side, right_side):
    return jnp.einsum("slk,skn->sln", left_side, right_side, preferred_element_type=jnp.float32)


def seq_dot_back(left_side, right_side):
    return jnp.einsum("sln,skn->slk", left_side, right_side, preferred_element_type=jnp.float32)


def seq_outer(left_side, right_side):
    return jnp.einsum("slk,sln->skn", left_side, right_side, preferred_element_type=jnp.float32)


def dot_back(left_side, right_side):
    return lax.dot_general(
        left_side, right_side, (((1,), (1,)), ((), ())), preferred_element_type=jnp.float32
    )


def widen_rows(low_rows):
    seq_total = low_rows.shape[0]
    identity = jnp.eye(seq_total, dtype=low_rows.dtype)
    widened = jnp.einsum("slr,st->sltr", low_rows, identity)
    return widened.reshape(seq_total * low_rows.shape[1], seq_total * low_rows.shape[2])


def block_scores(queries, keys_all, slopes, offset, block_rows):
    length = keys_all.shape[0]
    row_ids = offset + jnp.arange(block_rows)
    distance = (row_ids[:, None] - jnp.arange(length)[None, :]).astype(jnp.float32)
    query_block = lax.dynamic_slice_in_dim(queries, offset, block_rows, 0)
    raw_scores = jnp.einsum(
        "qhe,khe->hqk", query_block, keys_all, preferred_element_type=jnp.float32
    )
    scaled = (raw_scores - slopes[:, None, None] * distance[None]) * 0.125
    return (jnp.where(distance[None] >= 0, scaled, MASKED), query_block)


def attend(queries, keys_all, values_all, slopes, block_rows):
    length = queries.shape[0]

    def one_block(block_index):
        scores, _ = block_scores(queries, keys_all, slopes, block_index * block_rows, block_rows)
        row_max = jnp.max(scores, axis=-1, keepdims=True)
        exp_scores = jnp.exp(scores - row_max)
        row_sum = jnp.sum(exp_scores, axis=-1, keepdims=True)
        attn_probs = (exp_scores / row_sum).astype(jnp.bfloat16)
        context = jnp.einsum(
            "hqk,khe->qhe", attn_probs, values_all, preferred_element_type=jnp.float32
        )
        return (context.astype(jnp.bfloat16), (row_max + jnp.log(row_sum))[..., 0])

    context, log_sums = lax.map(one_block, jnp.arange(length // block_rows))
    return (context.reshape(queries.shape), log_sums)


def attend_back(queries, keys_all, values_all, grad_context, log_sums, slopes, block_rows):
    length = queries.shape[0]

    def one_block(running, block_index):
        grad_keys, grad_values = running
        offset = block_index * block_rows
        scores, query_block = block_scores(queries, keys_all, slopes, offset, block_rows)
        grad_block = lax.dynamic_slice_in_dim(grad_context, offset, block_rows, 0)
        attn_probs = jnp.exp(scores - log_sums[block_index][:, :, None])
        grad_probs = jnp.einsum(
            "qhe,khe->hqk", grad_block, values_all, preferred_element_type=jnp.float32
        )
        row_dot = jnp.sum(attn_probs * grad_probs, axis=-1, keepdims=True)
        grad_scores = (attn_probs * (grad_probs - row_dot)).astype(jnp.bfloat16)
        grad_queries = (
            jnp.einsum("hqk,khe->qhe", grad_scores, keys_all, preferred_element_type=jnp.float32)
            * 0.125
        )
        grad_keys = (
            grad_keys
            + jnp.einsum(
                "hqk,qhe->khe", grad_scores, query_block, preferred_element_type=jnp.float32
            )
            * 0.125
        )
        grad_values = grad_values + jnp.einsum(
            "hqk,qhe->khe",
            attn_probs.astype(jnp.bfloat16),
            grad_block,
            preferred_element_type=jnp.float32,
        )
        return ((grad_keys, grad_values), grad_queries)

    zeros_kv = jnp.zeros(keys_all.shape, jnp.float32)
    (grad_keys, grad_values), grad_queries = lax.scan(
        one_block, (zeros_kv, zeros_kv), jnp.arange(length // block_rows)
    )
    return (grad_queries.reshape(queries.shape), grad_keys, grad_values)


def local(
    tokens,
    grad_out,
    adapter_ids,
    first_gain,
    first_shift,
    joined_weight,
    joined_bias,
    dense_weight,
    dense_bias,
    second_gain,
    second_shift,
    up_weight,
    up_bias,
    down_weight,
    down_bias,
    joined_adapt_in,
    joined_adapt_out,
    dense_adapt_in,
    dense_adapt_out,
    up_adapt_in,
    up_adapt_out,
    down_adapt_in,
    down_adapt_out,
):
    local_rows = tokens.shape[0]
    model_width = tokens.shape[1]
    seq_total = adapter_ids.shape[0]
    group_rows = local_rows * lax.axis_size("tp")
    length = group_rows // seq_total
    block_rows = min(512, length)
    set_count = joined_adapt_in.shape[0]
    low_rank = joined_adapt_in.shape[2]
    joined_width = joined_bias.shape[0]
    hidden_width = up_bias.shape[0]
    local_heads = joined_width // (3 * HEAD_DIM)
    head_cols = local_heads * HEAD_DIM
    head_ids = lax.axis_index("tp") * local_heads + jnp.arange(local_heads)
    slopes = jnp.exp2(-8.0 * (head_ids + 1).astype(jnp.float32) / HEADS)
    matches = adapter_ids[:, None] == jnp.arange(set_count)[None, :]
    onehot_low = matches.astype(jnp.bfloat16)
    onehot_high = matches.astype(jnp.float32)
    pick_joined_in = choose(onehot_low, joined_adapt_in)
    pick_joined_out = choose(onehot_low, joined_adapt_out)
    pick_dense_in = choose(onehot_low, dense_adapt_in)
    pick_dense_out = choose(onehot_low, dense_adapt_out)
    pick_up_in = choose(onehot_low, up_adapt_in)
    pick_up_out = choose(onehot_low, up_adapt_out)
    pick_down_in = choose(onehot_low, down_adapt_in)
    pick_down_out = choose(onehot_low, down_adapt_out)
    residual_in = tokens.astype(jnp.float32)
    normed_one = layer_norm(residual_in, first_gain, first_shift).astype(jnp.bfloat16)
    gathered_one = lax.all_gather(normed_one, "tp", axis=0, tiled=True)
    w_joined, w_dense = (
        lax.all_gather(joined_weight, "fsdp", axis=0, tiled=True),
        lax.all_gather(dense_weight, "fsdp", axis=1, tiled=True),
    )
    seq_one = gathered_one.reshape(seq_total, length, model_width)
    low_joined = seq_dot(seq_one, pick_joined_in).astype(jnp.bfloat16)
    joined_cols = jnp.dot(gathered_one, w_joined, preferred_element_type=jnp.float32).reshape(
        seq_total, length, joined_width
    )
    joined_cols = (joined_cols + seq_dot(low_joined, pick_joined_out) + joined_bias).astype(
        jnp.bfloat16
    )
    joined_heads = joined_cols.reshape(seq_total, length, local_heads, 3, HEAD_DIM)
    sequence = 0
    context, log_sums = attend(
        joined_heads[sequence, :, :, 0, :],
        joined_heads[sequence, :, :, 1, :],
        joined_heads[sequence, :, :, 2, :],
        slopes,
        block_rows,
    )
    contexts = [context]
    log_list = [log_sums]
    seq_context = jnp.stack(contexts).reshape(seq_total, length, head_cols)
    context_rows = seq_context.reshape(group_rows, head_cols)
    low_dense = seq_dot(seq_context, pick_dense_in).astype(jnp.bfloat16)
    wide_dense = widen_rows(low_dense)
    stack_dense = pick_dense_out.reshape(seq_total * low_rank, model_width)
    rows_low = wide_dense
    attn_sum = sum_at_owner(
        (
            jnp.dot(context_rows, w_dense, preferred_element_type=jnp.float32)
            + jnp.dot(rows_low, stack_dense, preferred_element_type=jnp.float32)
        ).astype(jnp.bfloat16),
        "tp",
        0,
    )
    residual_mid = residual_in + attn_sum + dense_bias
    normed_two = layer_norm(residual_mid, second_gain, second_shift).astype(jnp.bfloat16)
    gathered_two = lax.all_gather(normed_two, "tp", axis=0, tiled=True)
    w_up, w_down = (
        lax.all_gather(up_weight, "fsdp", axis=0, tiled=True),
        lax.all_gather(down_weight, "fsdp", axis=1, tiled=True),
    )
    seq_two = gathered_two.reshape(seq_total, length, model_width)
    low_up = seq_dot(seq_two, pick_up_in).astype(jnp.bfloat16)
    pre_act = (
        jnp.dot(gathered_two, w_up, preferred_element_type=jnp.float32)
        + seq_dot(low_up, pick_up_out).reshape(group_rows, hidden_width)
        + up_bias
    )
    activated = exact_gelu(pre_act).astype(jnp.bfloat16)
    seq_act = activated.reshape(seq_total, length, hidden_width)
    low_down = seq_dot(seq_act, pick_down_in).astype(jnp.bfloat16)
    wide_down = widen_rows(low_down)
    stack_down = pick_down_out.reshape(seq_total * low_rank, model_width)
    rows_low = wide_down
    mlp_sum = sum_at_owner(
        (
            jnp.dot(activated, w_down, preferred_element_type=jnp.float32)
            + jnp.dot(rows_low, stack_down, preferred_element_type=jnp.float32)
        ).astype(jnp.bfloat16),
        "tp",
        0,
    )
    layer_out = (residual_mid + mlp_sum + down_bias).astype(jnp.bfloat16)
    grad_mlp = lax.all_gather(grad_out, "tp", axis=0, tiled=True)
    back_up, back_down = (w_up, w_down)
    seq_grad_mlp = grad_mlp.reshape(seq_total, length, model_width)
    grad_low_down = seq_dot_back(seq_grad_mlp, pick_down_out).astype(jnp.bfloat16)
    term_down_out = seq_outer(low_down, seq_grad_mlp)
    term_down_in = seq_outer(seq_act, grad_low_down)
    grad_act = dot_back(grad_mlp, back_down) + seq_dot_back(grad_low_down, pick_down_in).reshape(
        group_rows, hidden_width
    )
    _, gelu_pull = jax.vjp(exact_gelu, pre_act)
    grad_pre = gelu_pull(grad_act)[0].astype(jnp.bfloat16)
    seq_grad_pre = grad_pre.reshape(seq_total, length, hidden_width)
    grad_low_up = seq_dot_back(seq_grad_pre, pick_up_out).astype(jnp.bfloat16)
    term_up_out = seq_outer(low_up, seq_grad_pre)
    term_up_in = seq_outer(seq_two, grad_low_up)
    wide_up = widen_rows(grad_low_up)
    stack_up = jnp.swapaxes(pick_up_in, 1, 2).reshape(seq_total * low_rank, model_width)
    rows_grad = grad_pre
    rows_low = wide_up
    grad_norm_two = sum_at_owner(
        (
            dot_back(rows_grad, back_up)
            + jnp.dot(rows_low, stack_up, preferred_element_type=jnp.float32)
        ).astype(jnp.bfloat16),
        "tp",
        0,
    )
    _, norm_pull_two = jax.vjp(
        lambda rows_in: layer_norm(rows_in, second_gain, second_shift), residual_mid
    )
    grad_mid = grad_out.astype(jnp.float32) + norm_pull_two(grad_norm_two)[0]
    grad_attn = lax.all_gather(grad_mid.astype(jnp.bfloat16), "tp", axis=0, tiled=True)
    back_joined, back_dense = (w_joined, w_dense)
    seq_grad_attn = grad_attn.reshape(seq_total, length, model_width)
    grad_low_dense = seq_dot_back(seq_grad_attn, pick_dense_out).astype(jnp.bfloat16)
    term_dense_out = seq_outer(low_dense, seq_grad_attn)
    term_dense_in = seq_outer(seq_context, grad_low_dense)
    grad_context = dot_back(grad_attn, back_dense) + seq_dot_back(
        grad_low_dense, pick_dense_in
    ).reshape(group_rows, head_cols)
    grad_context = grad_context.astype(jnp.bfloat16).reshape(
        seq_total, length, local_heads, HEAD_DIM
    )
    sequence = 0
    grad_query, grad_key, grad_value = attend_back(
        joined_heads[sequence, :, :, 0, :],
        joined_heads[sequence, :, :, 1, :],
        joined_heads[sequence, :, :, 2, :],
        grad_context[sequence],
        log_list[sequence],
        slopes,
        block_rows,
    )
    grad_parts = [jnp.stack((grad_query, grad_key, grad_value), axis=2)]
    grad_joined = (
        jnp.stack(grad_parts).astype(jnp.bfloat16).reshape(seq_total, length, joined_width)
    )
    grad_low_joined = seq_dot_back(grad_joined, pick_joined_out).astype(jnp.bfloat16)
    term_joined_out = seq_outer(low_joined, grad_joined)
    term_joined_in = seq_outer(seq_one, grad_low_joined)
    grad_joined_rows = grad_joined.reshape(group_rows, joined_width)
    wide_joined = widen_rows(grad_low_joined)
    stack_joined = jnp.swapaxes(pick_joined_in, 1, 2).reshape(seq_total * low_rank, model_width)
    rows_grad = grad_joined_rows
    rows_low = wide_joined
    grad_norm_one = sum_at_owner(
        (
            dot_back(rows_grad, back_joined)
            + jnp.dot(rows_low, stack_joined, preferred_element_type=jnp.float32)
        ).astype(jnp.bfloat16),
        "tp",
        0,
    )
    _, norm_pull_one = jax.vjp(
        lambda rows_in: layer_norm(rows_in, first_gain, first_shift), residual_in
    )
    grad_tokens = grad_mid + norm_pull_one(grad_norm_one)[0]
    wide_sums = tuple(
        (
            part.astype(jnp.float32)
            for part in together(
                (
                    spread(onehot_high, term_joined_out).astype(jnp.bfloat16),
                    spread(onehot_high, term_dense_in).astype(jnp.bfloat16),
                    spread(onehot_high, term_up_out).astype(jnp.bfloat16),
                    spread(onehot_high, term_down_in).astype(jnp.bfloat16),
                ),
                "fsdp",
            )
        )
    )
    both_sums = lax.psum(
        (
            spread(onehot_high, term_joined_in),
            spread(onehot_high, term_dense_out),
            spread(onehot_high, term_up_in),
            spread(onehot_high, term_down_out),
        ),
        ("fsdp", "tp"),
    )
    return (
        layer_out,
        grad_tokens,
        both_sums[0],
        wide_sums[0],
        wide_sums[1],
        both_sums[1],
        both_sums[2],
        wide_sums[2],
        wide_sums[3],
        both_sums[3],
    )


def solution(mesh):
    return jax.shard_map(
        local,
        mesh=mesh,
        in_specs=(
            P(("fsdp", "tp"), None),
            P(("fsdp", "tp"), None),
            P("fsdp"),
            P(),
            P(),
            P("fsdp", "tp"),
            P("tp"),
            P("tp", "fsdp"),
            P(),
            P(),
            P(),
            P("fsdp", "tp"),
            P("tp"),
            P("tp", "fsdp"),
            P(),
            P(),
            P(None, None, "tp"),
            P(None, "tp", None),
            P(),
            P(),
            P(None, None, "tp"),
            P(None, "tp", None),
            P(),
        ),
        out_specs=(
            P(("fsdp", "tp"), None),
            P(("fsdp", "tp"), None),
            P(),
            P(None, None, "tp"),
            P(None, "tp", None),
            P(),
            P(),
            P(None, None, "tp"),
            P(None, "tp", None),
            P(),
        ),
        check_vma=False,
    )
```

profile of v0, /device:TPU:1, one launch (start us, length us, event | category | flops | bytes accessed | tf_op | source)
XLA Modules:
  0.0 977.7 jit_solution(4659292120763606901)
XLA Ops:
  19.2 68.6 %all-gather.9.cloned.1.call-done = bf16[1024,2048]{1,0:T(8,128)(2,1)} async-done(((bf16[128,2048]{1,0:T(8,128)(2,1)}), bf16[1024,2048]{1,0:T(8,128)(2,1)}) %all-gather.9.cloned.1.call-update) | async-done | bytes 4194320 | tf_op jit(solution)/shard_map/all_gather | solution.py:200
  91.2 32.7 %all-gather.11.cloned.1.call-done = bf16[2048,768]{1,0:T(8,128)(2,1)} async-done(((bf16[128,768]{1,0:T(8,128)(2,1)}), bf16[2048,768]{1,0:T(8,128)(2,1)}) %all-gather.11.cloned.1.call-update) | async-done | bytes 3145744 | tf_op jit(solution)/shard_map/all_gather | solution.py:202
  123.9 6.4 fusion.96
  131.2 22.1 %while.28 = (s32[]{:T(128)}, bf16[2,512,4,64]{1,3,2,0:T(8,128)(2,1)S(1)}, f32[2,4,512]{2,1,0:T(4,128)S(1)}, s32[2]{0:T(128)S(1)}, bf16[1024,4,64]{0,2,1:T(8,128)...) while((s32[]{:T(128)}, ...), condition=%wide.region_5.6_spmd.clone, body=%wide.region_2.5_spmd.clone.sunk | while | flops 577370624 | bytes 37297388 | solution.py:104
  138.8 3.4 fusion.189
  149.9 3.4 fusion.189
  154.2 5.4 all-gather.13.cloned.1.call-done
  163.4 62.2 %all_to_all.20 = bf16[8,128,2048]{2,1,0:T(8,128)(2,1)S(1)} all-to-all(bf16[8,128,2048]{2,1,0:T(8,128)(2,1)S(1)} %bitcast.233), channel_id=1, replica_groups=mesh['fsdp'=16,'tp'=8] {'tp'}, dimensions={0} | all-to-all | bytes 8388608 | tf_op jit(solution)/shard_map/all_to_all | solution.py:20
  232.0 33.0 %all-gather.21.cloned.1.call-done = bf16[1024,2048]{1,0:T(8,128)(2,1)} async-done(((bf16[128,2048]{1,0:T(8,128)(2,1)}), bf16[1024,2048]{1,0:T(8,128)(2,1)}) %all-gather.21.cloned.1.call-update) | async-done | bytes 4194320 | tf_op jit(solution)/shard_map/all_gather | solution.py:267
  268.3 41.9 %all-gather.19.cloned.1.call-done = bf16[1024,2048]{1,0:T(8,128)(2,1)} async-done(((bf16[1024,128]{1,0:T(8,128)(2,1)}), bf16[1024,2048]{1,0:T(8,128)(2,1)}) %all-gather.19.cloned.1.call-update) | async-done | bytes 4194320 | tf_op jit(solution)/shard_map/all_gather | solution.py:243
  310.2 10.0 %fusion.100 = f32[1024,1024]{1,0:T(8,128)} fusion(bf16[1024,2048]{1,0:T(8,128)(2,1)} %all-gather.21.cloned.1.call-done, bf16[1024,2048]{1,0:T(8,128)(2,1)} %all-gather.19.cloned.1.call-done), kind=kOutput, calls=%fused_computation.187 | convolution fusion | flops 4294967296 | bytes 12582912 | tf_op jit(solution)/shard_map/dot_general | solution.py:66
  320.2 63.6 %all-gather.15.cloned.1.call-done = bf16[1024,2048]{1,0:T(8,128)(2,1)} async-done(((bf16[128,2048]{1,0:T(8,128)(2,1)}), bf16[1024,2048]{1,0:T(8,128)(2,1)}) %all-gather.15.cloned.1.call-update) | async-done | bytes 4194320 | tf_op jit(solution)/shard_map/all_gather | solution.py:240
  387.2 34.3 %all-gather.17.cloned.1.call-done = bf16[2048,1024]{1,0:T(8,128)(2,1)} async-done(((bf16[128,1024]{1,0:T(8,128)(2,1)}), bf16[2048,1024]{1,0:T(8,128)(2,1)}) %all-gather.17.cloned.1.call-update) | async-done | bytes 4194320 | tf_op jit(solution)/shard_map/all_gather | solution.py:242
  421.5 7.9 fusion.98
  429.5 11.2 %multiply_convert_fusion.2 = (bf16[1024,1024]{1,0:T(8,128)(2,1)}, f32[1024,1024]{1,0:T(8,128)S(1)}, f32[1024,1024]{1,0:T(8,128)S(1)}) fusion(f32[1024]{0:T(1024)S(1)} %copy-done.56, f32[1024,1024]{1,0:T(8,128)S(1)} %fusion.98, bf16[1024,16]{0,1:T(8,128)(2,1)S(1)} %convolution_convert_fusion.4, bf16[1,16,1024]{2,0,1:T(2,128)(2,1)S(1)} %fusion.66), kind=kOutput, calls=%fused_computation.60 | convolution fusion | flops 103809024 | bytes 14749696 | tf_op jit(solution)/shard_map/slk,skn->sln/dot_general | solution.py:54
  443.6 4.6 fusion.101
  451.5 6.5 all-to-all-start.2
  460.2 6.9 fusion.99
  470.5 36.2 %all-to-all-done.2 = bf16[8,128,2048]{2,1,0:T(8,128)(2,1)} async-done(((bf16[8,128,2048]{2,1,0:T(8,128)(2,1)}), bf16[8,128,2048]{2,1,0:T(8,128)(2,1)}, u32[]{:S(2)}, u32[]{:S(2)}) %all-to-all-start.2) | async-done | bytes 4194336 | tf_op jit(solution)/shard_map/all_to_all | solution.py:20
  506.8 5.1 all-to-all-start.1
  515.2 45.4 %all-to-all-done.1 = bf16[8,128,2048]{2,1,0:T(8,128)(2,1)} async-done(((bf16[8,128,2048]{2,1,0:T(8,128)(2,1)}), bf16[8,128,2048]{2,1,0:T(8,128)(2,1)}, u32[]{:S(2)}, u32[]{:S(2)}) %all-to-all-start.1) | async-done | bytes 4194336 | tf_op jit(solution)/shard_map/all_to_all | solution.py:20
  576.9 3.7 fusion.109
  581.9 55.0 %all-gather.23.cloned.1.call-done = bf16[1024,2048]{1,0:T(8,128)(2,1)} async-done(((bf16[128,2048]{1,0:T(8,128)(2,1)}), bf16[1024,2048]{1,0:T(8,128)(2,1)}) %all-gather.23.cloned.1.call-update) | async-done | bytes 4194320 | tf_op jit(solution)/shard_map/all_gather | solution.py:298
  636.9 3.5 convolution_convert_fusion.1
  643.7 29.9 %while.29 = (s32[]{:T(128)}, f32[1024,4,64]{0,2,1:T(8,128)S(1)}, f32[1024,4,64]{0,2,1:T(8,128)S(1)}, bf16[2,512,4,64]{1,3,2,0:T(8,128)(2,1)}, s32[2]{0:T(128)S(1...) while((s32[]{:T(128)}, f32[1024,4,64]{0,2,1:T(8,128)S(1)}, ...), condition=%wide.region_15.16_spmd.clone, body=%wide.region_13.15_spmd.clone.sunk | while | flops 1369307648 | bytes 81836928 | solution.py:142
  650.3 3.9 multiply_reduce_fusion.4
  665.0 3.9 multiply_reduce_fusion.4
  679.0 5.4 fusion.103
  687.7 4.6 all-to-all-start.3
  699.3 101.2 %all-reduce.4.cloned.1.call-done = bf16[393216]{0:T(1024)(128)(2,1)} async-done(((bf16[393216]{0:T(1024)(128)(2,1)}), bf16[393216]{0:T(1024)(128)(2,1)}) %all-reduce.4.cloned.1.call-update) | async-done | bytes 786448 | tf_op jit(solution)/shard_map/psum | solution.py:28
  809.3 3.6 copy.47
  818.3 145.4 %all-reduce.6.cloned.1.call-done = (f32[8,2048,16]{1,2,0:T(8,128)}, f32[8,16,2048]{2,1,0:T(8,128)}, f32[8,2048,16]{1,2,0:T(8,128)}, f32[8,16,2048]{2,1,0:T(8,128)}) async-done(((f32[8,2048,16]{1,2,0:T(8,128)}, f32[8,16,2048]{2,1,0:T(8,128)}, f32[8,2048,16]{1,2,0:T(8,128)}, f32[8,16,2048]{2,1,0:T(8,128)}), (f32[8,2048,16]{1,2,0:T(8,128)}, f32[8,16,2048]{2,1,0:T(8,128)}, f32[8,2048,16]{1,2,0:T(8,128)}, ...) | async-done | bytes 4194320 | tf_op jit(solution)/shard_map/psum | solution.py:358
  (279 shorter events, 135.5 us)
Async XLA Ops:
  7.2 10.6 %copy-start = (bf16[8,2048,16]{1,2,0:T(8,128)(2,1)S(1)}, bf16[8,2048,16]{1,2,0:T(8,128)(2,1)}, u32[]{:S(2)}) copy-start(bf16[8,2048,16]{1,2,0:T(8,128)(2,1)} %param.42) | copy-start | bytes 1572868
  7.2 11.3 %copy-start.38 = (bf16[8,16,768]{2,1,0:T(8,128)(2,1)S(1)}, bf16[8,16,768]{2,1,0:T(8,128)(2,1)}, u32[]{:S(2)}) copy-start(bf16[8,16,768]{2,1,0:T(8,128)(2,1)} %param.43) | copy-start | bytes 589828
  7.2 11.5 %copy-start.24 = (bf16[8,16,2048]{2,1,0:T(8,128)(2,1)S(1)}, bf16[8,16,2048]{2,1,0:T(8,128)(2,1)}, u32[]{:S(2)}) copy-start(bf16[8,16,2048]{2,1,0:T(8,128)(2,1)} %param.45) | copy-start | bytes 1572868
  7.2 80.6 %all-gather.9.cloned.1.call-start = ((), (), s32[]{:S(2)}) async-start(), calls=%async_computation.4 | async-start | bytes 4718592 | tf_op jit(solution)/shard_map/all_gather | solution.py:200
  13.3 110.7 %all-gather.11.cloned.1.call-start = ((), (), s32[]{:S(2)}) async-start(), calls=%async_computation.5 | async-start | bytes 3342336 | tf_op jit(solution)/shard_map/all_gather | solution.py:202
  14.0 145.6 %all-gather.13.cloned.1.call-start = ((), (), s32[]{:S(2)}) async-start(), calls=%async_computation.6 | async-start | bytes 1114112 | tf_op jit(solution)/shard_map/all_gather | solution.py:203
  14.7 250.2 %all-gather.21.cloned.1.call-start = ((), (), s32[]{:S(2)}) async-start(), calls=%async_computation.10 | async-start | bytes 4718592 | tf_op jit(solution)/shard_map/all_gather | solution.py:267
  15.3 294.9 %all-gather.19.cloned.1.call-start = ((), (), s32[]{:S(2)}) async-start(), calls=%async_computation.9 | async-start | bytes 4456448 | tf_op jit(solution)/shard_map/all_gather | solution.py:243
  15.9 367.9 %all-gather.15.cloned.1.call-start = ((), (), s32[]{:S(2)}) async-start(), calls=%async_computation.7 | async-start | bytes 4718592 | tf_op jit(solution)/shard_map/all_gather | solution.py:240
  18.5 72.6 %copy-start.14 = (bf16[1,2048,16]{2,1,0:T(8,128)(2,1)}, bf16[1,2048,16]{2,1,0:T(8,128)(2,1)S(1)}, u32[]{:S(2)}) copy-start(bf16[1,2048,16]{2,1,0:T(8,128)(2,1)S(1)} %copy.49) | copy-start | bytes 196612
  18.7 111.6 %copy-start.36 = (bf16[1,16,768]{2,0,1:T(2,128)(2,1)}, bf16[1,16,768]{2,0,1:T(2,128)(2,1)S(1)}, u32[]{:S(2)}) copy-start(bf16[1,16,768]{2,0,1:T(2,128)(2,1)S(1)} %fusion.68) | copy-start | bytes 73732
  19.2 142.9 %copy-start.28 = (bf16[1,16,2048]{2,0,1:T(2,128)(2,1)}, bf16[1,16,2048]{2,0,1:T(2,128)(2,1)S(1)}, u32[]{:S(2)}) copy-start(bf16[1,16,2048]{2,0,1:T(2,128)(2,1)S(1)} %fusion.60) | copy-start | bytes 196612
  91.1 39.2 %copy-start.30 = (bf16[1024,16]{0,1:T(8,128)(2,1)}, bf16[1024,16]{0,1:T(8,128)(2,1)S(1)}, u32[]{:S(2)}) copy-start(bf16[1024,16]{0,1:T(8,128)(2,1)S(1)} %convolution_convert_fusion.5) | copy-start | bytes 98308
  91.1 39.2 %copy-start.50 = (f32[768]{0:T(1024)S(1)}, f32[768]{0:T(1024)}, u32[]{:S(2)}) copy-start(f32[768]{0:T(1024)} %param.33) | copy-start | bytes 9220
  153.3 8.8 copy-start.8
  153.9 8.2 copy-start.11
  154.2 8.0 copy-start.32
  228.3 193.3 %all-gather.17.cloned.1.call-start = ((), (), s32[]{:S(2)}) async-start(), calls=%async_computation.8 | async-start | bytes 4456448 | tf_op jit(solution)/shard_map/all_gather | solution.py:242
  387.2 42.3 %copy-start.56 = (f32[1024]{0:T(1024)S(1)}, f32[1024]{0:T(1024)}, u32[]{:S(2)}) copy-start(f32[1024]{0:T(1024)} %param.39) | copy-start | bytes 12292
  429.5 11.2 %copy-start.57 = (f32[1024,1024]{1,0:T(8,128)S(1)}, f32[1024,1024]{1,0:T(8,128)}, u32[]{:S(2)}) copy-start(f32[1024,1024]{1,0:T(8,128)} %fusion.100) | copy-start | bytes 12582916
  451.5 55.3 %all-to-all-start.2 = ((bf16[8,128,2048]{2,1,0:T(8,128)(2,1)}), bf16[8,128,2048]{2,1,0:T(8,128)(2,1)}, u32[]{:S(2)}, u32[]{:S(2)}) async-start(bf16[8,128,2048]{2,1,0:T(8,128)(2,1)} %bitcast.232), calls=%async_computation.2 | async-start | bytes 8388608 | tf_op jit(solution)/shard_map/all_to_all | solution.py:20
  506.8 53.8 %all-to-all-start.1 = ((bf16[8,128,2048]{2,1,0:T(8,128)(2,1)}), bf16[8,128,2048]{2,1,0:T(8,128)(2,1)}, u32[]{:S(2)}, u32[]{:S(2)}) async-start(bf16[8,128,2048]{2,1,0:T(8,128)(2,1)} %bitcast.231), calls=%async_computation.1 | async-start | bytes 8388608 | tf_op jit(solution)/shard_map/all_to_all | solution.py:20
  511.8 125.0 %all-gather.23.cloned.1.call-start = ((), (), s32[]{:S(2)}) async-start(), calls=%async_computation.11 | async-start | bytes 4718592 | tf_op jit(solution)/shard_map/all_gather | solution.py:298
  514.9 48.7 %copy-start.47 = (f32[2048]{0:T(1024)S(1)}, f32[2048]{0:T(1024)}, u32[]{:S(2)}) copy-start(f32[2048]{0:T(1024)} %param.41) | copy-start | bytes 24580
  566.8 233.7 %all-reduce.4.cloned.1.call-start = ((), (), s32[]{:S(2)}) async-start(), calls=%async_computation.12 | async-start | bytes 1572864 | tf_op jit(solution)/shard_map/psum | solution.py:28
  687.7 125.2 %all-to-all-start.3 = ((bf16[8,128,2048]{2,1,0:T(8,128)(2,1)}), bf16[8,128,2048]{2,1,0:T(8,128)(2,1)}, u32[]{:S(2)}, u32[]{:S(2)}) async-start(bf16[8,128,2048]{2,1,0:T(8,128)(2,1)} %bitcast.230), calls=%async_computation.3 | async-start | bytes 8388608 | tf_op jit(solution)/shard_map/all_to_all | solution.py:20
  692.3 271.4 %all-reduce.6.cloned.1.call-start = ((), (), s32[]{:S(2)}) async-start(), calls=%async_computation.13 | async-start | bytes 8388608 | tf_op jit(solution)/shard_map/psum | solution.py:358
  809.3 6.7 copy-start.4
  809.3 6.7 copy-start.39
  809.3 6.7 copy-start.44
  963.7 5.7 copy-start.19
  963.7 6.7 copy-start.1
  (42 other events, 111.3 us)
Sparse Core Ops, SparseCore 0:
  13.4 74.3 all-gather.8
  89.5 34.3 all-gather.10
  125.5 33.9 all-gather.12
  161.8 103.1 all-gather.20
  266.4 43.7 all-gather.18
  313.0 70.7 all-gather.14
  385.6 35.9 all-gather.16
  566.9 69.9 all-gather.22
  679.1 121.3 all-reduce.3
  807.4 156.1 all-reduce.5
where the time goes:
time: 982 us; the launch traced here: 978 us
  waiting for transfers between devices  666 us (68%)
  matrix products  139 us (14%)
  blocking collectives  62.2 us (6%)
  other arithmetic  40.9 us (4%)
  local copies, waits for them, and re-layouts  29.7 us (3%)
  starting transfers between devices  16.5 us (2%)
  between operations  16.2 us (2%)
    psum x1, waiting for transfers between devices, local(): lax.psum((spread(onehot_high, term_joined_in), spread(onehot_high, term_d...  145 us
    psum x1, waiting for transfers between devices, together(): so_far = lax.psum(jnp.concatenate([a.ravel() for a in arrays]), axis)  101 us
    all_to_all x3, waiting for transfers between devices, sum_at_owner(): lax.all_to_all(blocks, axis, split_axis=0, concat_axis=0, tiled=True)  81.6 us
    all_gather x1, waiting for transfers between devices, local(): gathered_one = lax.all_gather(normed_one, 'tp', axis=0, tiled=True)  68.6 us
    all_gather x1, waiting for transfers between devices, local(): gathered_two = lax.all_gather(normed_two, 'tp', axis=0, tiled=True)  63.6 us
    all_to_all x1, blocking collectives, sum_at_owner(): lax.all_to_all(blocks, axis, split_axis=0, concat_axis=0, tiled=True)  62.2 us
    all_gather x1, waiting for transfers between devices, local(): lax.all_gather(grad_mid.astype(jnp.bfloat16), 'tp', axis=0, tiled=True)  55 us
    all_gather x1, waiting for transfers between devices, local(): lax.all_gather(down_weight, 'fsdp', axis=1, tiled=True)  41.9 us
  transfers between devices with their start and end apart: 13, of which 12 were waited for; matrix products, arithmetic and copies ran while one was open for 13% of the time, Pallas kernels for 0%

commit v1 on v0

--- a/solution.py
+++ b/solution.py
@@ -356,13 +356,16 @@
         )
     )
     both_sums = lax.psum(
-        (
-            spread(onehot_high, term_joined_in),
-            spread(onehot_high, term_dense_out),
-            spread(onehot_high, term_up_in),
-            spread(onehot_high, term_down_out),
+        lax.psum(
+            (
+                spread(onehot_high, term_joined_in),
+                spread(onehot_high, term_dense_out),
+                spread(onehot_high, term_up_in),
+                spread(onehot_high, term_down_out),
+            ),
+            "tp",
         ),
-        ("fsdp", "tp"),
+        "fsdp",
     )
     return (
         layer_out,

time: 982 us -> 1060 us (1.079)
  waiting for transfers between devices: 666 us -> 748 us
    psum x0 -> x1, waiting for transfers between devices: none -> 114 us  [local(): lax.psum(lax.psum((spread(onehot_high, term_joined_in), spread(onehot_hig...]
    psum x1, waiting for transfers between devices: 145 us -> 115 us  [local(): lax.psum((spread(onehot_high, term_joined_in), spread(onehot_high, term_d...]
  transfers between devices with their start and end apart: 13 -> 14, of which waited for: 12 -> 13; matrix products, arithmetic and copies ran while one was open for 13% -> 12% of each run, Pallas kernels for 0% -> 0%
where the time goes in v1:
time: 1060 us
  waiting for transfers between devices  748 us (71%)
  matrix products  139 us (13%)
  blocking collectives  62.2 us (6%)
  other arithmetic  40.9 us (4%)
  local copies, waits for them, and re-layouts  28.5 us (3%)
  starting transfers between devices  16.8 us (2%)
  between operations  15.9 us (2%)
    psum x1, waiting for transfers between devices, local(): lax.psum((spread(onehot_high, term_joined_in), spread(onehot_high, term_d...  115 us
    psum x1, waiting for transfers between devices, local(): lax.psum(lax.psum((spread(onehot_high, term_joined_in), spread(onehot_hig...  114 us
    psum x1, waiting for transfers between devices, together(): so_far = lax.psum(jnp.concatenate([a.ravel() for a in arrays]), axis)  100 us
    all_to_all x3, waiting for transfers between devices, sum_at_owner(): lax.all_to_all(blocks, axis, split_axis=0, concat_axis=0, tiled=True)  81.6 us
    all_gather x1, waiting for transfers between devices, local(): gathered_one = lax.all_gather(normed_one, 'tp', axis=0, tiled=True)  68.5 us
    all_gather x1, waiting for transfers between devices, local(): gathered_two = lax.all_gather(normed_two, 'tp', axis=0, tiled=True)  63.6 us
    all_to_all x1, blocking collectives, sum_at_owner(): lax.all_to_all(blocks, axis, split_axis=0, concat_axis=0, tiled=True)  62.2 us
    all_gather x1, waiting for transfers between devices, local(): lax.all_gather(grad_mid.astype(jnp.bfloat16), 'tp', axis=0, tiled=True)  55 us
  transfers between devices with their start and end apart: 14, of which 13 were waited for; matrix products, arithmetic and copies ran while one was open for 12% of the time, Pallas kernels for 0%

profile of v1, /device:TPU:1, one launch (start us, length us, event | category | flops | bytes accessed | tf_op | source)
XLA Modules:
  0.0 1058.3 jit_solution(17858091058051564245)
XLA Ops:
  18.2 68.5 %all-gather.9.cloned.1.call-done = bf16[1024,2048]{1,0:T(8,128)(2,1)} async-done(((bf16[128,2048]{1,0:T(8,128)(2,1)}), bf16[1024,2048]{1,0:T(8,128)(2,1)}) %all-gather.9.cloned.1.call-update) | async-done | bytes 4194320 | tf_op jit(solution)/shard_map/all_gather | solution.py:200
  90.1 32.7 %all-gather.11.cloned.1.call-done = bf16[2048,768]{1,0:T(8,128)(2,1)} async-done(((bf16[128,768]{1,0:T(8,128)(2,1)}), bf16[2048,768]{1,0:T(8,128)(2,1)}) %all-gather.11.cloned.1.call-update) | async-done | bytes 3145744 | tf_op jit(solution)/shard_map/all_gather | solution.py:202
  122.9 6.4 fusion.96
  130.1 22.1 %while.28 = (s32[]{:T(128)}, bf16[2,512,4,64]{1,3,2,0:T(8,128)(2,1)S(1)}, f32[2,4,512]{2,1,0:T(4,128)S(1)}, s32[2]{0:T(128)S(1)}, bf16[1024,4,64]{0,2,1:T(8,128)...) while((s32[]{:T(128)}, ...), condition=%wide.region_5.6_spmd.clone, body=%wide.region_2.5_spmd.clone.sunk | while | flops 577370624 | bytes 37297388 | solution.py:104
  148.8 3.4 fusion.189
  153.1 5.4 all-gather.13.cloned.1.call-done
  162.4 62.2 %all_to_all.20 = bf16[8,128,2048]{2,1,0:T(8,128)(2,1)S(1)} all-to-all(bf16[8,128,2048]{2,1,0:T(8,128)(2,1)S(1)} %bitcast.233), channel_id=1, replica_groups=mesh['fsdp'=16,'tp'=8] {'tp'}, dimensions={0} | all-to-all | bytes 8388608 | tf_op jit(solution)/shard_map/all_to_all | solution.py:20
  231.0 32.9 %all-gather.21.cloned.1.call-done = bf16[1024,2048]{1,0:T(8,128)(2,1)} async-done(((bf16[128,2048]{1,0:T(8,128)(2,1)}), bf16[1024,2048]{1,0:T(8,128)(2,1)}) %all-gather.21.cloned.1.call-update) | async-done | bytes 4194320 | tf_op jit(solution)/shard_map/all_gather | solution.py:267
  267.3 41.9 %all-gather.19.cloned.1.call-done = bf16[1024,2048]{1,0:T(8,128)(2,1)} async-done(((bf16[1024,128]{1,0:T(8,128)(2,1)}), bf16[1024,2048]{1,0:T(8,128)(2,1)}) %all-gather.19.cloned.1.call-update) | async-done | bytes 4194320 | tf_op jit(solution)/shard_map/all_gather | solution.py:243
  309.2 10.0 fusion.100
  319.2 63.6 %all-gather.15.cloned.1.call-done = bf16[1024,2048]{1,0:T(8,128)(2,1)} async-done(((bf16[128,2048]{1,0:T(8,128)(2,1)}), bf16[1024,2048]{1,0:T(8,128)(2,1)}) %all-gather.15.cloned.1.call-update) | async-done | bytes 4194320 | tf_op jit(solution)/shard_map/all_gather | solution.py:240
  386.2 34.3 %all-gather.17.cloned.1.call-done = bf16[2048,1024]{1,0:T(8,128)(2,1)} async-done(((bf16[128,1024]{1,0:T(8,128)(2,1)}), bf16[2048,1024]{1,0:T(8,128)(2,1)}) %all-gather.17.cloned.1.call-update) | async-done | bytes 4194320 | tf_op jit(solution)/shard_map/all_gather | solution.py:242
  420.5 8.0 fusion.98
  428.4 11.2 %multiply_convert_fusion.2 = (bf16[1024,1024]{1,0:T(8,128)(2,1)}, f32[1024,1024]{1,0:T(8,128)S(1)}, f32[1024,1024]{1,0:T(8,128)S(1)}) fusion(f32[1024]{0:T(1024)S(1)} %copy-done.56, f32[1024,1024]{1,0:T(8,128)S(1)} %fusion.98, bf16[1024,16]{0,1:T(8,128)(2,1)S(1)} %convolution_convert_fusion.4, bf16[1,16,1024]{2,0,1:T(2,128)(2,1)S(1)} %fusion.66), kind=kOutput, calls=%fused_computation.60 | convolution fusion | flops 103809024 | bytes 14749696 | tf_op jit(solution)/shard_map/slk,skn->sln/dot_general | solution.py:54
  442.6 4.6 fusion.101
  450.4 6.5 all-to-all-start.2
  459.2 6.9 fusion.99
  469.5 36.2 %all-to-all-done.2 = bf16[8,128,2048]{2,1,0:T(8,128)(2,1)} async-done(((bf16[8,128,2048]{2,1,0:T(8,128)(2,1)}), bf16[8,128,2048]{2,1,0:T(8,128)(2,1)}, u32[]{:S(2)}, u32[]{:S(2)}) %all-to-all-start.2) | async-done | bytes 4194336 | tf_op jit(solution)/shard_map/all_to_all | solution.py:20
  505.7 5.1 all-to-all-start.1
  514.2 45.4 %all-to-all-done.1 = bf16[8,128,2048]{2,1,0:T(8,128)(2,1)} async-done(((bf16[8,128,2048]{2,1,0:T(8,128)(2,1)}), bf16[8,128,2048]{2,1,0:T(8,128)(2,1)}, u32[]{:S(2)}, u32[]{:S(2)}) %all-to-all-start.1) | async-done | bytes 4194336 | tf_op jit(solution)/shard_map/all_to_all | solution.py:20
  575.9 3.7 fusion.109
  580.9 55.0 %all-gather.23.cloned.1.call-done = bf16[1024,2048]{1,0:T(8,128)(2,1)} async-done(((bf16[128,2048]{1,0:T(8,128)(2,1)}), bf16[1024,2048]{1,0:T(8,128)(2,1)}) %all-gather.23.cloned.1.call-update) | async-done | bytes 4194320 | tf_op jit(solution)/shard_map/all_gather | solution.py:298
  635.9 3.5 convolution_convert_fusion.1
  642.7 29.7 %while.29 = (s32[]{:T(128)}, f32[1024,4,64]{0,2,1:T(8,128)S(1)}, f32[1024,4,64]{0,2,1:T(8,128)S(1)}, bf16[2,512,4,64]{1,3,2,0:T(8,128)(2,1)}, s32[2]{0:T(128)S(1...) while((s32[]{:T(128)}, f32[1024,4,64]{0,2,1:T(8,128)S(1)}, ...), condition=%wide.region_15.16_spmd.clone, body=%wide.region_13.15_spmd.clone.sunk | while | flops 1369307648 | bytes 81836928 | solution.py:142
  649.2 3.9 multiply_reduce_fusion.4
  663.9 3.9 multiply_reduce_fusion.4
  685.0 5.4 fusion.103
  693.7 4.6 all-to-all-start.3
  698.4 100.2 %all-reduce.6.cloned.1.call-done = bf16[393216]{0:T(1024)(128)(2,1)} async-done(((bf16[393216]{0:T(1024)(128)(2,1)}), bf16[393216]{0:T(1024)(128)(2,1)}) %all-reduce.6.cloned.1.call-update) | async-done | bytes 786448 | tf_op jit(solution)/shard_map/psum | solution.py:28
  799.6 114.6 %all-reduce.10.cloned.1.call-done = (f32[8,2048,16]{1,2,0:T(8,128)}, f32[8,16,2048]{2,1,0:T(8,128)}, f32[8,2048,16]{1,2,0:T(8,128)}, f32[8,16,2048]{2,1,0:T(8,128)}) async-done(((f32[8,2048,16]{1,2,0:T(8,128)}, f32[8,16,2048]{2,1,0:T(8,128)}, f32[8,2048,16]{1,2,0:T(8,128)}, f32[8,16,2048]{2,1,0:T(8,128)}), (f32[8,2048,16]{1,2,0:T(8,128)}, f32[8,16,2048]{2,1,0:T(8,128)}, f32[8,2048,16]{1,2,0:T(8,128)}, ...) | async-done | bytes 4194320 | tf_op jit(solution)/shard_map/psum | solution.py:359
  921.7 3.6 copy.47
  930.7 113.9 %all-reduce.8.cloned.1.call-done = (f32[8,2048,16]{1,2,0:T(8,128)}, f32[8,16,2048]{2,1,0:T(8,128)}, f32[8,2048,16]{1,2,0:T(8,128)}, f32[8,16,2048]{2,1,0:T(8,128)}) async-done(((f32[8,2048,16]{1,2,0:T(8,128)}, f32[8,16,2048]{2,1,0:T(8,128)}, f32[8,2048,16]{1,2,0:T(8,128)}, f32[8,16,2048]{2,1,0:T(8,128)}), (f32[8,2048,16]{1,2,0:T(8,128)}, f32[8,16,2048]{2,1,0:T(8,128)}, f32[8,2048,16]{1,2,0:T(8,128)}, ...) | async-done | bytes 4194320 | tf_op jit(solution)/shard_map/psum | solution.py:358
  (282 shorter events, 137.9 us)
Async XLA Ops:
  7.2 9.5 copy-start
  7.2 10.3 copy-start.38
  7.2 10.5 copy-start.24
  7.2 79.5 %all-gather.9.cloned.1.call-start = ((), (), s32[]{:S(2)}) async-start(), calls=%async_computation.4 | async-start | bytes 4718592 | tf_op jit(solution)/shard_map/all_gather | solution.py:200
  8.5 8.1 copy-start.43
  9.9 6.8 copy-start.53
  9.9 6.8 copy-start.48
  12.2 110.7 %all-gather.11.cloned.1.call-start = ((), (), s32[]{:S(2)}) async-start(), calls=%async_computation.5 | async-start | bytes 3342336 | tf_op jit(solution)/shard_map/all_gather | solution.py:202
  12.9 145.6 %all-gather.13.cloned.1.call-start = ((), (), s32[]{:S(2)}) async-start(), calls=%async_computation.6 | async-start | bytes 1114112 | tf_op jit(solution)/shard_map/all_gather | solution.py:203
  13.7 250.2 %all-gather.21.cloned.1.call-start = ((), (), s32[]{:S(2)}) async-start(), calls=%async_computation.10 | async-start | bytes 4718592 | tf_op jit(solution)/shard_map/all_gather | solution.py:267
  14.3 294.9 %all-gather.19.cloned.1.call-start = ((), (), s32[]{:S(2)}) async-start(), calls=%async_computation.9 | async-start | bytes 4456448 | tf_op jit(solution)/shard_map/all_gather | solution.py:243
  14.8 368.0 %all-gather.15.cloned.1.call-start = ((), (), s32[]{:S(2)}) async-start(), calls=%async_computation.7 | async-start | bytes 4718592 | tf_op jit(solution)/shard_map/all_gather | solution.py:240
  17.5 72.6 %copy-start.14 = (bf16[1,2048,16]{2,1,0:T(8,128)(2,1)}, bf16[1,2048,16]{2,1,0:T(8,128)(2,1)S(1)}, u32[]{:S(2)}) copy-start(bf16[1,2048,16]{2,1,0:T(8,128)(2,1)S(1)} %copy.49) | copy-start | bytes 196612
  17.7 111.6 %copy-start.36 = (bf16[1,16,768]{2,0,1:T(2,128)(2,1)}, bf16[1,16,768]{2,0,1:T(2,128)(2,1)S(1)}, u32[]{:S(2)}) copy-start(bf16[1,16,768]{2,0,1:T(2,128)(2,1)S(1)} %fusion.68) | copy-start | bytes 73732
  18.2 142.9 %copy-start.28 = (bf16[1,16,2048]{2,0,1:T(2,128)(2,1)}, bf16[1,16,2048]{2,0,1:T(2,128)(2,1)S(1)}, u32[]{:S(2)}) copy-start(bf16[1,16,2048]{2,0,1:T(2,128)(2,1)S(1)} %fusion.60) | copy-start | bytes 196612
  90.1 39.2 %copy-start.30 = (bf16[1024,16]{0,1:T(8,128)(2,1)}, bf16[1024,16]{0,1:T(8,128)(2,1)S(1)}, u32[]{:S(2)}) copy-start(bf16[1024,16]{0,1:T(8,128)(2,1)S(1)} %convolution_convert_fusion.5) | copy-start | bytes 98308
  90.1 39.2 %copy-start.50 = (f32[768]{0:T(1024)S(1)}, f32[768]{0:T(1024)}, u32[]{:S(2)}) copy-start(f32[768]{0:T(1024)} %param.33) | copy-start | bytes 9220
  152.2 8.8 copy-start.8
  152.9 8.2 copy-start.11
  153.1 8.0 copy-start.32
  227.2 193.2 %all-gather.17.cloned.1.call-start = ((), (), s32[]{:S(2)}) async-start(), calls=%async_computation.8 | async-start | bytes 4456448 | tf_op jit(solution)/shard_map/all_gather | solution.py:242
  386.2 42.3 %copy-start.56 = (f32[1024]{0:T(1024)S(1)}, f32[1024]{0:T(1024)}, u32[]{:S(2)}) copy-start(f32[1024]{0:T(1024)} %param.39) | copy-start | bytes 12292
  428.4 11.2 %copy-start.57 = (f32[1024,1024]{1,0:T(8,128)S(1)}, f32[1024,1024]{1,0:T(8,128)}, u32[]{:S(2)}) copy-start(f32[1024,1024]{1,0:T(8,128)} %fusion.100) | copy-start | bytes 12582916
  450.4 55.3 %all-to-all-start.2 = ((bf16[8,128,2048]{2,1,0:T(8,128)(2,1)}), bf16[8,128,2048]{2,1,0:T(8,128)(2,1)}, u32[]{:S(2)}, u32[]{:S(2)}) async-start(bf16[8,128,2048]{2,1,0:T(8,128)(2,1)} %bitcast.232), calls=%async_computation.2 | async-start | bytes 8388608 | tf_op jit(solution)/shard_map/all_to_all | solution.py:20
  505.7 53.8 %all-to-all-start.1 = ((bf16[8,128,2048]{2,1,0:T(8,128)(2,1)}), bf16[8,128,2048]{2,1,0:T(8,128)(2,1)}, u32[]{:S(2)}, u32[]{:S(2)}) async-start(bf16[8,128,2048]{2,1,0:T(8,128)(2,1)} %bitcast.231), calls=%async_computation.1 | async-start | bytes 8388608 | tf_op jit(solution)/shard_map/all_to_all | solution.py:20
  510.8 125.0 %all-gather.23.cloned.1.call-start = ((), (), s32[]{:S(2)}) async-start(), calls=%async_computation.11 | async-start | bytes 4718592 | tf_op jit(solution)/shard_map/all_gather | solution.py:298
  513.9 48.7 %copy-start.47 = (f32[2048]{0:T(1024)S(1)}, f32[2048]{0:T(1024)}, u32[]{:S(2)}) copy-start(f32[2048]{0:T(1024)} %param.41) | copy-start | bytes 24580
  565.8 232.8 %all-reduce.6.cloned.1.call-start = ((), (), s32[]{:S(2)}) async-start(), calls=%async_computation.12 | async-start | bytes 1572864 | tf_op jit(solution)/shard_map/psum | solution.py:28
  677.8 236.5 %all-reduce.10.cloned.1.call-start = ((), (), s32[]{:S(2)}) async-start(), calls=%async_computation.14 | async-start | bytes 8388608 | tf_op jit(solution)/shard_map/psum | solution.py:359
  693.7 231.6 %all-to-all-start.3 = ((bf16[8,128,2048]{2,1,0:T(8,128)(2,1)}), bf16[8,128,2048]{2,1,0:T(8,128)(2,1)}, u32[]{:S(2)}, u32[]{:S(2)}) async-start(bf16[8,128,2048]{2,1,0:T(8,128)(2,1)} %bitcast.230), calls=%async_computation.3 | async-start | bytes 8388608 | tf_op jit(solution)/shard_map/all_to_all | solution.py:20
  698.3 346.3 %all-reduce.8.cloned.1.call-start = ((), (), s32[]{:S(2)}) async-start(), calls=%async_computation.13 | async-start | bytes 8388608 | tf_op jit(solution)/shard_map/psum | solution.py:358
  921.7 6.7 copy-start.44
  (43 other events, 137.4 us)
Sparse Core Ops, SparseCore 0:
  12.3 74.3 all-gather.8
  88.4 34.3 all-gather.10
  124.5 33.9 all-gather.12
  160.7 103.1 all-gather.20
  265.4 43.7 all-gather.18
  312.0 70.7 all-gather.14
  384.5 35.9 all-gather.16
  565.9 69.9 all-gather.22
  677.9 120.6 all-reduce.5
  801.9 112.2 all-reduce.9
  917.2 127.3 all-reduce.7
